TPU v7x, 512 devices: a whole 4x8x8 slice. The times are simulated.
512 devices in a mesh: ctx: 64 (over y, z), tp: 8 (over x, core).
Axes of the slice: x: 4, y: 8, z: 8, core: 2. Of those that a mesh axis runs over, the one named last changes fastest.
Arguments:
- query: bfloat16 [8192, 8192], P('ctx', 'tp'), may hold values from -6 to 6
- keyed: bfloat16 [8192, 8192], P('ctx', 'tp'), may hold values from -6 to 6
- valued: bfloat16 [8192, 8192], P('ctx', 'tp'), may hold values from -6 to 6
- short_taps: float32 [3, 3, 8192], P(None, None, 'tp'), may hold values from -3.5 to 3.5
- rates: float32 [8, 8192], P(None, 'tp'), may hold values from 3.0517578e-05 to 0.1
- residues: float32 [8, 8192], P(None, 'tp'), may hold values from -1.5 to 1.5
- skip_gain: float32 [8192], P('tp'), may hold values from -1.6 to 1.6
- doc_ids: int32 [8192], P('ctx'), may hold values from 0 to 7, never falling along the last dimension, each value on 1 to 4096 neighbouring positions
Outputs:
- mixed: bfloat16 [8192, 8192], P('ctx', 'tp')
Inputs may be any that keep to these rules, and one draw needn't show every extreme that they name: doc_ids never falls along the sequence; each of the 8 documents holds 1 to 4096 consecutive tokens, one exactly 4096.
All inputs are finite; a program needn't handle non-finite values.
Results may differ from a plain program's by a relative error of at most 0.0065.
Values may be sent and summed in bfloat16 or wider, within the bound.
A program may use at most 128 MiB of HBM per device.

v0:
```python
import jax
import jax.numpy as jnp
from jax import lax
from jax.sharding import PartitionSpec as P


def shifted_2(value, axis, steps):
    count = lax.axis_size(axis)
    first, last = (max(0, -steps), min(count, count - steps))
    return lax.ppermute(value, axis, [(source, source + steps) for source in range(first, last)])


def short_conv(ext, ids_ext, taps):
    width = taps.shape[1] - 1
    length = ext.shape[1] - width
    total = jnp.zeros((ext.shape[0], length, ext.shape[2]), jnp.float32)
    for tap in range(taps.shape[1]):
        seg = ext[:, width - tap : width - tap + length]
        same = (ids_ext[width - tap : width - tap + length] == ids_ext[width:]).astype(jnp.float32)
        total = total + taps[:, tap][:, None, :] * seg * same[None, :, None]
    return total


def mode_terms_all(gated, ids, rates, residues):
    block, channels = gated.shape
    order = rates.shape[0]
    places = jnp.arange(block, dtype=jnp.float32)
    shifted = places - float(block // 2)
    lower = places[:, None] >= places[None, :]
    mask = (lower & (ids[:, None] == ids[None, :])).astype(jnp.float32)
    grow = jnp.exp(rates[None] * shifted[:, None, None])
    weighted = (grow * gated[:, None, :]).reshape(block, order * channels)
    summed = jnp.dot(mask, weighted, precision=lax.Precision.HIGHEST).reshape(
        block, order, channels
    )
    states = summed * jnp.exp(-rates[None] * shifted[:, None, None])
    long_part = jnp.sum(residues[None] * states, axis=1)
    return (long_part, states[block - 1])


def incoming(carry, ids, prev_last, rates, residues):
    block = ids.shape[0]
    places = jnp.arange(block, dtype=jnp.float32) + 1.0
    live = (ids == prev_last).astype(jnp.float32)
    total = jnp.zeros((block, rates.shape[1]), jnp.float32)
    for group in range(rates.shape[0] // 4):
        rate = rates[4 * group : 4 * group + 4]
        weight = residues[4 * group : 4 * group + 4] * carry[4 * group : 4 * group + 4]
        total = total + jnp.sum(weight[None] * jnp.exp(-rate[None] * places[:, None, None]), axis=1)
    return total * live[:, None]


def transition(ids, prev_last, rates):
    block = ids.shape[0]
    keep = ((ids[0] == prev_last) & (ids[0] == ids[block - 1])).astype(jnp.float32)
    return jnp.exp(-rates * block) * keep


def combine(earlier, later):
    return (earlier[0] * later[0], later[0] * earlier[1] + later[1])


def on_device(query, keyed, valued, short_taps, rates, residues, skip_gain, doc_ids):
    block, channels = query.shape
    width = short_taps.shape[1] - 1
    stacked = jnp.stack([query, keyed, valued])
    prev_rows, prev_ids = shifted_2(
        (stacked[:, block - width :], doc_ids[block - width :]), "ctx", 1
    )
    ext = jnp.concatenate([prev_rows, stacked], axis=1).astype(jnp.float32)
    ids_ext = jnp.concatenate([prev_ids, doc_ids])
    conv = short_conv(ext, ids_ext, short_taps)
    gated = (conv[1] * conv[2]).astype(jnp.bfloat16)
    gated_f = gated.astype(jnp.float32)
    n_ctx = lax.axis_size("ctx")
    group_width = channels // n_ctx
    whole = lax.all_to_all(gated, "ctx", split_axis=1, concat_axis=0, tiled=True)
    ids_all = lax.all_gather(doc_ids, "ctx", axis=0, tiled=True)
    offset = lax.axis_index("ctx") * group_width
    rate_sub = lax.dynamic_slice_in_dim(rates, offset, group_width, 1)
    resid_sub = lax.dynamic_slice_in_dim(residues, offset, group_width, 1)
    blocks_u = whole.reshape(n_ctx, block, group_width).astype(jnp.float32)
    blocks_ids = ids_all.reshape(n_ctx, block)
    prev_lasts = jnp.concatenate([jnp.zeros((1,), jnp.int32), blocks_ids[:-1, block - 1]])
    local_parts, ends = jax.vmap(lambda uu, ii: mode_terms_all(uu, ii, rate_sub, resid_sub))(
        blocks_u, blocks_ids
    )
    keeps = jax.vmap(lambda ii, pp: transition(ii, pp, rate_sub))(blocks_ids, prev_lasts)
    _, inclusive = lax.associative_scan(combine, (keeps, ends), axis=0)
    carries = jnp.concatenate([jnp.zeros_like(inclusive[:1]), inclusive[:-1]], axis=0)
    entering = jax.vmap(lambda cc, ii, pp: incoming(cc, ii, pp, rate_sub, resid_sub))(
        carries, blocks_ids, prev_lasts
    )
    grouped = (local_parts + entering).reshape(n_ctx * block, group_width)
    long_all = lax.all_to_all(grouped, "ctx", split_axis=0, concat_axis=1, tiled=True)
    return (conv[0] * (long_all + skip_gain[None] * gated_f)).astype(jnp.bfloat16)


def solution(mesh):
    return jax.shard_map(
        on_device,
        mesh=mesh,
        in_specs=(
            P("ctx", "tp"),
            P("ctx", "tp"),
            P("ctx", "tp"),
            P(None, None, "tp"),
            P(None, "tp"),
            P(None, "tp"),
            P("tp"),
            P("ctx"),
        ),
        out_specs=P("ctx", "tp"),
        check_vma=False,
    )
```

profile of v0, /device:TPU:4, one launch (start us, length us, event | category | flops | bytes accessed | tf_op | source)
XLA Modules:
  0.0 192.9 jit_solution(2154041682382078537)
XLA Ops:
  0.0 1.1 copy.45
  1.2 1.1 copy.44
  2.3 1.1 copy.43
  3.4 0.3 pad_maximum_fusion
  3.7 0.3 copy.46
  4.0 4.3 %collective-permute-start = (bf16[3,2,1024]{2,1,0:T(2,128)(2,1)S(1)}, bf16[3,2,1024]{2,1,0:T(2,128)(2,1)S(1)}, u32[]{:S(2)}, u32[]{:S(2)}) collective-permute-start(bf16[3,2,1024]{2,1,0:T(2,128)(2,1)S(1)} %copy.46), channel_id=1, source_target_pairs={{0,8},{8,16},{16,24},{24,32},{32,40},{40,48},{48,56},{56,64},{64,7... | collective-permute-start | bytes 36872 | tf_op jit(solution)/shard_map/ppermute | solution.py:10
  8.3 0.1 slice.217
  8.4 4.3 %collective-permute-start.1 = (s32[2]{0:T(128)S(1)}, s32[2]{0:T(128)S(1)}, u32[]{:S(2)}, u32[]{:S(2)}) collective-permute-start(s32[2]{0:T(128)S(1)} %slice.217), channel_id=1, source_target_pairs={{0,8},{8,16},{16,24},{24,32},{32,40},{40,48},{48,56},{56,64},{64,7... | collective-permute-start | bytes 32 | tf_op jit(solution)/shard_map/ppermute | solution.py:10
  12.7 0.8 multiply_exponential_fusion.4
  13.4 0.1 mul.302
  13.5 47.9 %all-gather = s32[64,1,128]{2,1,0:T(1,128)S(1)} all-gather(s32[1,1,128]{2,1,0:T(1,128)S(1)} %bitcast.48), channel_id=1, replica_groups=mesh['ctx'=64,'tp'=8] {'ctx'}, dimensions={0}, use_global_device_ids=true | all-gather | bytes 33280 | tf_op jit(solution)/shard_map/all_gather | solution.py:78
  61.4 0.2 slice_reduce_fusion
  61.6 0.2 slice_reduce_fusion.1
  61.9 0.1 constant_dynamic-slice_fusion.1
  61.9 0.1 pad_add_fusion.2
  62.0 0.1 compare_convert_fusion
  62.1 0.1 multiply_exponential_fusion.1
  62.2 0.1 and_convert_fusion
  62.3 0.1 multiply_exponential_fusion.2
  62.4 0.1 pad_add_fusion.1
  62.5 0.1 compare_convert_fusion.2
  62.5 0.4 copy.47
  63.0 0.6 maximum_convert_fusion
  63.6 2.3 %fusion.7 = f32[3,128,1024]{1,2,0:T(8,128)S(1)} fusion(f32[3,130,1024]{1,2,0:T(8,128)S(1)} %maximum_convert_fusion, f32[128]{0:T(128)S(1)} %get-tuple-element.36, f32[3,1024]{1,0:T(4,128)S(1)} %get-tuple-element.39, f32[128]{0:T(128)S(1)} %get-tuple-element.35, f32[3,1024]{1,0:T(4,128)S(1)} %get-tuple-element.40, f32[3,1024]{1,0:T(4,128)S(1)} %bitcast.47), kind=kLoop, calls=%fused_computation.13 | loop fusion | flops 2752512 | bytes 6329344 | tf_op jit(solution)/shard_map/add | solution.py:20
  65.9 0.8 fusion.10
  66.7 8.1 %all-to-all-start = ((bf16[128,64,16]{0,2,1:T(8,128)(2,1)}), bf16[128,64,16]{0,2,1:T(8,128)(2,1)S(1)}, u32[]{:S(2)}, u32[]{:S(2)}) async-start(bf16[128,64,16]{0,2,1:T(8,128)(2,1)} %bitcast.6), calls=%async_computation | async-start | bytes 524288 | tf_op jit(solution)/shard_map/all_to_all | solution.py:77
  74.9 0.1 broadcast_multiply_fusion.1
  75.0 0.2 multiply_exponential_fusion
  75.2 13.0 %all-to-all-done = bf16[128,64,16]{0,2,1:T(8,128)(2,1)S(1)} async-done(((bf16[128,64,16]{0,2,1:T(8,128)(2,1)}), bf16[128,64,16]{0,2,1:T(8,128)(2,1)S(1)}, u32[]{:S(2)}, u32[]{:S(2)}) %all-to-all-start) | async-done | bytes 262176 | tf_op jit(solution)/shard_map/all_to_all | solution.py:77
  88.3 0.6 bitcast_multiply_fusion
  88.9 6.1 %fusion = f32[64,128,128]{1,2,0:T(8,128)} fusion(f32[64,128,128]{1,2,0:T(8,128)S(1)} %bitcast_multiply_fusion, s32[64,128]{1,0:T(8,128)S(1)} %bitcast.46, pred[128,128]{1,0:T(8,128)(4,1)S(1)} %iota_compare_fusion), kind=kOutput, calls=%fused_computation.3 | convolution fusion | flops 1612709888 | bytes 8437760 | tf_op jit(solution)/shard_map/vmap()/dot_general | solution.py:33
  95.0 16.9 %copy.48 = f32[64,128,8,16]{3,2,1,0:T(8,128)} copy(f32[64,128,8,16]{1,3,2,0:T(8,128)} %bitcast.36) | data formatting | bytes 8388608 | tf_op jit(solution)/shard_map/vmap()/reshape | solution.py:33
  111.9 53.4 %multiply_reduce_fusion = (f32[64,128,16]{2,1,0:T(8,128)}, f32[64,128,8,16]{3,2,1,0:T(8,128)}) fusion(f32[8,16]{1,0:T(8,128)S(1)} %constant_dynamic-slice_fusion.1, f32[64,128,8,16]{3,2,1,0:T(8,128)} %copy.48, f32[128,8,16]{2,1,0:T(8,128)S(1)} %multiply_exponential_fusion), kind=kLoop, calls=%fused_computation | loop fusion | flops 3014656 | bytes 8978944 | tf_op jit(solution)/shard_map/vmap()/reduce_sum | solution.py:37
  165.3 1.0 slice_bitcast_fusion.1
  166.7 0.1 pad.44
  166.8 0.1 pad.45
  166.9 0.7 slice_bitcast_fusion.2
  167.6 0.1 pad.47
  167.7 0.1 pad.46
  167.9 2.8 %copy.49 = f32[64,128,16]{1,2,0:T(8,128)S(1)} copy(f32[64,128,16]{2,1,0:T(8,128)} %get-tuple-element.9) | data formatting | bytes 1048576 | tf_op jit(solution)/shard_map/vmap()/reduce_sum | solution.py:37
  170.7 0.2 pad.75
  171.0 0.2 pad.116
  171.3 0.6 multiply_reduce_fusion.2
  171.9 0.6 multiply_reduce_fusion.1
  172.6 0.1 multiply_add_fusion
  172.7 19.1 %all_to_all.26 = f32[64,128,16]{1,2,0:T(8,128)S(1)} all-to-all(f32[64,128,16]{1,2,0:T(8,128)S(1)} %multiply_add_fusion), channel_id=1, replica_groups=mesh['ctx'=64,'tp'=8] {'ctx'}, dimensions={0} | all-to-all | bytes 1048576 | tf_op jit(solution)/shard_map/all_to_all | solution.py:95
  191.8 0.2 fusion.12
  192.1 0.9 copy.50
  (52 shorter events, 0.6 us)
Async XLA Ops:
  0.0 61.8 %copy-start = (f32[8,1024]{1,0:T(8,128)S(1)}, f32[8,1024]{1,0:T(8,128)}, u32[]{:S(2)}) copy-start(f32[8,1024]{1,0:T(8,128)} %param.13) | copy-start | bytes 98308
  0.0 8.3 %copy-start.3 = (s32[128]{0:T(128)S(1)}, s32[128]{0:T(128)}, u32[]{:S(2)}) copy-start(s32[128]{0:T(128)} %param.15) | copy-start | bytes 1540
  0.0 61.8 %copy-start.2 = (f32[3,3,1024]{2,1,0:T(4,128)S(1)}, f32[3,3,1024]{2,1,0:T(4,128)}, u32[]{:S(2)}) copy-start(f32[3,3,1024]{2,1,0:T(4,128)} %param.11) | copy-start | bytes 110596
  4.0 58.5 %collective-permute-start = (bf16[3,2,1024]{2,1,0:T(2,128)(2,1)S(1)}, bf16[3,2,1024]{2,1,0:T(2,128)(2,1)S(1)}, u32[]{:S(2)}, u32[]{:S(2)}) collective-permute-start(bf16[3,2,1024]{2,1,0:T(2,128)(2,1)S(1)} %copy.46), channel_id=1, source_target_pairs={{0,8},{8,16},{16,24},{24,32},{32,40},{40,48},{48,56},{56,64},{64,7... | collective-permute-start | bytes 36872 | tf_op jit(solution)/shard_map/ppermute | solution.py:10
  8.4 54.0 %collective-permute-start.1 = (s32[2]{0:T(128)S(1)}, s32[2]{0:T(128)S(1)}, u32[]{:S(2)}, u32[]{:S(2)}) collective-permute-start(s32[2]{0:T(128)S(1)} %slice.217), channel_id=1, source_target_pairs={{0,8},{8,16},{16,24},{24,32},{32,40},{40,48},{48,56},{56,64},{64,7... | collective-permute-start | bytes 32 | tf_op jit(solution)/shard_map/ppermute | solution.py:10
  66.7 21.6 %all-to-all-start = ((bf16[128,64,16]{0,2,1:T(8,128)(2,1)}), bf16[128,64,16]{0,2,1:T(8,128)(2,1)S(1)}, u32[]{:S(2)}, u32[]{:S(2)}) async-start(bf16[128,64,16]{0,2,1:T(8,128)(2,1)} %bitcast.6), calls=%async_computation | async-start | bytes 524288 | tf_op jit(solution)/shard_map/all_to_all | solution.py:77
  171.9 19.9 %copy-start.4 = (f32[1024]{0:T(1024)S(1)}, f32[1024]{0:T(1024)}, u32[]{:S(2)}) copy-start(f32[1024]{0:T(1024)} %param.14) | copy-start | bytes 12292
  172.6 20.4 %copy-start.1 = (f32[8,1024]{1,0:T(8,128)S(1)}, f32[8,1024]{1,0:T(8,128)}, u32[]{:S(2)}) copy-start(f32[8,1024]{1,0:T(8,128)} %param.13) | copy-start | bytes 98308
where the time goes:
time: 194 us; the launch traced here: 193 us
  blocking collectives  67 us (35%)
  other arithmetic  61.6 us (32%)
  local copies, waits for them, and re-layouts  27.9 us (14%)
  starting transfers between devices  16.7 us (9%)
  waiting for transfers between devices  13 us (7%)
  matrix products  6.12 us (3%)
    reduce_sum x1, other arithmetic, mode_terms_all(): long_part = jnp.sum(residues[None] * states, axis=1)  53.4 us
    all_gather x1, blocking collectives, on_device(): ids_all = lax.all_gather(doc_ids, 'ctx', axis=0, tiled=True)  47.9 us
    all_to_all x1, blocking collectives, on_device(): lax.all_to_all(grouped, 'ctx', split_axis=0, concat_axis=1, tiled=True)  19.1 us
    reshape x1, local copies, waits for them, and re-layouts, mode_terms_all(): jnp.dot(mask, weighted, precision=lax.Precision.HIGHEST)  16.9 us
    all_to_all x1, waiting for transfers between devices, on_device(): lax.all_to_all(gated, 'ctx', split_axis=1, concat_axis=0, tiled=True)  13 us
    ppermute x2, starting transfers between devices, shifted_2(): lax.ppermute(value, axis, [(source, source + steps) for source in range(f...  8.54 us
    all_to_all x1, starting transfers between devices, on_device(): lax.all_to_all(gated, 'ctx', split_axis=1, concat_axis=0, tiled=True)  8.13 us
    dot_general x1, matrix products, mode_terms_all(): jnp.dot(mask, weighted, precision=lax.Precision.HIGHEST)  6.12 us
  transfers between devices with their start and end apart: 3, of which 1 were waited for; matrix products, arithmetic and copies ran while one was open for 1% of the time, Pallas kernels for 0%

commit v1 on v0

--- a/solution.py
+++ b/solution.py
@@ -75,7 +75,10 @@
     n_ctx = lax.axis_size("ctx")
     group_width = channels // n_ctx
     whole = lax.all_to_all(gated, "ctx", split_axis=1, concat_axis=0, tiled=True)
-    ids_all = lax.all_gather(doc_ids, "ctx", axis=0, tiled=True)
+    _expand_streams = lambda t0: jnp.concatenate(
+        lax.all_to_all(jnp.stack([t0 for _ in range(lax.axis_size("ctx"))], axis=0), "ctx", 0, 0), 0
+    )
+    ids_all = _expand_streams(doc_ids)
     offset = lax.axis_index("ctx") * group_width
     rate_sub = lax.dynamic_slice_in_dim(rates, offset, group_width, 1)
     resid_sub = lax.dynamic_slice_in_dim(residues, offset, group_width, 1)

time: 194 us -> 168 us (0.87)
  the two profiles are of different devices: /device:TPU:4 before, /device:TPU:2 now
where the time goes in v1:
time: 168 us; the launch traced here: 167 us
  other arithmetic  61.6 us (37%)
  starting transfers between devices  30 us (18%)
  local copies, waits for them, and re-layouts  28.5 us (17%)
  blocking collectives  21.4 us (13%)
  waiting for transfers between devices  19.2 us (11%)
  matrix products  6.11 us (4%)
    reduce_sum x1, other arithmetic, mode_terms_all(): long_part = jnp.sum(residues[None] * states, axis=1)  53.4 us
    all_to_all x1, blocking collectives, on_device(): lax.all_to_all(grouped, 'ctx', split_axis=0, concat_axis=1, tiled=True)  21.4 us
    reshape x1, local copies, waits for them, and re-layouts, mode_terms_all(): jnp.dot(mask, weighted, precision=lax.Precision.HIGHEST)  16.9 us
    all_to_all x1, starting transfers between devices, on_device(): lax.all_to_all(jnp.stack([t0 for _ in range(lax.axis_size('ctx'))], axis=...  14.8 us
    all_to_all x1, waiting for transfers between devices, on_device(): lax.all_to_all(gated, 'ctx', split_axis=1, concat_axis=0, tiled=True)  13.1 us
    ppermute x2, starting transfers between devices, shifted_2(): lax.ppermute(value, axis, [(source, source + steps) for source in range(f...  8.54 us
    all_to_all x1, starting transfers between devices, on_device(): lax.all_to_all(gated, 'ctx', split_axis=1, concat_axis=0, tiled=True)  6.72 us
    all_to_all x1, waiting for transfers between devices, on_device(): lax.all_to_all(jnp.stack([t0 for _ in range(lax.axis_size('ctx'))], axis=...  6.16 us
  transfers between devices with their start and end apart: 4, of which 2 were waited for; matrix products, arithmetic and copies ran while one was open for 4% of the time, Pallas kernels for 0%

profile of v1, /device:TPU:2, one launch (start us, length us, event | category | flops | bytes accessed | tf_op | source)
XLA Modules:
  0.0 167.5 jit_solution(15131963026310935058)
XLA Ops:
  0.0 1.1 copy.57
  1.2 1.1 copy.56
  2.3 1.1 copy.55
  3.4 0.3 pad_maximum_fusion
  3.7 0.3 copy.58
  4.0 4.3 %collective-permute-start = (bf16[3,2,1024]{2,1,0:T(2,128)(2,1)S(1)}, bf16[3,2,1024]{2,1,0:T(2,128)(2,1)S(1)}, u32[]{:S(2)}, u32[]{:S(2)}) collective-permute-start(bf16[3,2,1024]{2,1,0:T(2,128)(2,1)S(1)} %copy.58), channel_id=1, source_target_pairs={{0,8},{8,16},{16,24},{24,32},{32,40},{40,48},{48,56},{56,64},{64,7... | collective-permute-start | bytes 36872 | tf_op jit(solution)/shard_map/ppermute | solution.py:10
  8.3 0.1 slice.217
  8.4 4.3 %collective-permute-start.1 = (s32[2]{0:T(128)S(1)}, s32[2]{0:T(128)S(1)}, u32[]{:S(2)}, u32[]{:S(2)}) collective-permute-start(s32[2]{0:T(128)S(1)} %slice.217), channel_id=1, source_target_pairs={{0,8},{8,16},{16,24},{24,32},{32,40},{40,48},{48,56},{56,64},{64,7... | collective-permute-start | bytes 32 | tf_op jit(solution)/shard_map/ppermute | solution.py:10
  12.7 0.6 stack.14
  13.3 14.8 %all-to-all-start = ((s32[64,1,128]{2,1,0:T(1,128)}), s32[64,1,128]{2,1,0:T(1,128)S(1)}, u32[]{:S(2)}, u32[]{:S(2)}) async-start(s32[64,1,128]{2,1,0:T(1,128)} %stack.14), calls=%async_computation | async-start | bytes 65536 | tf_op jit(solution)/shard_map/all_to_all | solution.py:79
  28.1 0.8 multiply_exponential_fusion.4
  28.9 0.1 mul.302
  29.1 0.1 constant_dynamic-slice_fusion.1
  29.1 0.1 multiply_exponential_fusion.1
  29.2 0.2 multiply_exponential_fusion
  29.5 0.1 multiply_exponential_fusion.2
  29.6 0.1 pad_add_fusion.1
  29.7 0.1 compare_convert_fusion.2
  29.8 0.4 copy.59
  30.2 0.6 maximum_convert_fusion
  30.8 2.3 %fusion.7 = f32[3,128,1024]{1,2,0:T(8,128)S(1)} fusion(f32[3,130,1024]{1,2,0:T(8,128)S(1)} %maximum_convert_fusion, f32[128]{0:T(128)S(1)} %get-tuple-element.36, f32[3,1024]{1,0:T(4,128)S(1)} %get-tuple-element.39, f32[128]{0:T(128)S(1)} %get-tuple-element.35, f32[3,1024]{1,0:T(4,128)S(1)} %get-tuple-element.40, f32[3,1024]{1,0:T(4,128)S(1)} %bitcast.46), kind=kLoop, calls=%fused_computation.13 | loop fusion | flops 2752512 | bytes 6329344 | tf_op jit(solution)/shard_map/add | solution.py:20
  33.1 0.8 fusion.10
  33.9 6.2 %all-to-all-done = s32[64,1,128]{2,1,0:T(1,128)S(1)} async-done(((s32[64,1,128]{2,1,0:T(1,128)}), s32[64,1,128]{2,1,0:T(1,128)S(1)}, u32[]{:S(2)}, u32[]{:S(2)}) %all-to-all-start) | async-done | bytes 32800 | tf_op jit(solution)/shard_map/all_to_all | solution.py:79
  40.0 6.7 %all-to-all-start.1 = ((bf16[128,64,16]{0,2,1:T(8,128)(2,1)}), bf16[128,64,16]{0,2,1:T(8,128)(2,1)S(1)}, u32[]{:S(2)}, u32[]{:S(2)}) async-start(bf16[128,64,16]{0,2,1:T(8,128)(2,1)} %bitcast.5), calls=%async_computation.1 | async-start | bytes 524288 | tf_op jit(solution)/shard_map/all_to_all | solution.py:77
  46.8 0.2 slice_reduce_fusion
  47.0 0.2 slice_reduce_fusion.1
  47.1 0.1 and_convert_fusion
  47.2 0.1 pad_add_fusion.2
  47.3 0.1 compare_convert_fusion
  47.4 0.1 broadcast_multiply_fusion.1
  47.5 13.1 %all-to-all-done.1 = bf16[128,64,16]{0,2,1:T(8,128)(2,1)S(1)} async-done(((bf16[128,64,16]{0,2,1:T(8,128)(2,1)}), bf16[128,64,16]{0,2,1:T(8,128)(2,1)S(1)}, u32[]{:S(2)}, u32[]{:S(2)}) %all-to-all-start.1) | async-done | bytes 262176 | tf_op jit(solution)/shard_map/all_to_all | solution.py:77
  60.6 0.6 bitcast_multiply_fusion
  61.2 6.1 %fusion = f32[64,128,128]{1,2,0:T(8,128)} fusion(f32[64,128,128]{1,2,0:T(8,128)S(1)} %bitcast_multiply_fusion, s32[64,128]{1,0:T(8,128)S(1)} %bitcast.45, pred[128,128]{1,0:T(8,128)(4,1)S(1)} %iota_compare_fusion), kind=kOutput, calls=%fused_computation.3 | convolution fusion | flops 1612709888 | bytes 8437760 | tf_op jit(solution)/shard_map/vmap()/dot_general | solution.py:33
  67.3 16.9 %copy.60 = f32[64,128,8,16]{3,2,1,0:T(8,128)} copy(f32[64,128,8,16]{1,3,2,0:T(8,128)} %bitcast.35) | data formatting | bytes 8388608 | tf_op jit(solution)/shard_map/vmap()/reshape | solution.py:33
  84.2 53.4 %multiply_reduce_fusion = (f32[64,128,16]{2,1,0:T(8,128)}, f32[64,128,8,16]{3,2,1,0:T(8,128)}) fusion(f32[8,16]{1,0:T(8,128)S(1)} %constant_dynamic-slice_fusion.1, f32[64,128,8,16]{3,2,1,0:T(8,128)} %copy.60, f32[128,8,16]{2,1,0:T(8,128)S(1)} %multiply_exponential_fusion), kind=kLoop, calls=%fused_computation | loop fusion | flops 3014656 | bytes 8978944 | tf_op jit(solution)/shard_map/vmap()/reduce_sum | solution.py:37
  137.6 1.0 slice_bitcast_fusion.1
  139.2 0.7 slice_bitcast_fusion.2
  139.9 0.1 pad.47
  140.0 0.1 pad.46
  140.2 2.8 %copy.61 = f32[64,128,16]{1,2,0:T(8,128)S(1)} copy(f32[64,128,16]{2,1,0:T(8,128)} %get-tuple-element.9) | data formatting | bytes 1048576 | tf_op jit(solution)/shard_map/vmap()/reduce_sum | solution.py:37
  143.0 0.2 pad.75
  143.3 0.2 pad.116
  143.6 0.6 multiply_reduce_fusion.2
  144.2 0.6 multiply_reduce_fusion.1
  144.9 0.1 multiply_add_fusion
  145.0 21.4 %all_to_all.32 = f32[64,128,16]{1,2,0:T(8,128)S(1)} all-to-all(f32[64,128,16]{1,2,0:T(8,128)S(1)} %multiply_add_fusion), channel_id=1, replica_groups=mesh['ctx'=64,'tp'=8] {'ctx'}, dimensions={0} | all-to-all | bytes 1048576 | tf_op jit(solution)/shard_map/all_to_all | solution.py:98
  166.4 0.2 fusion.12
  166.6 0.9 copy.62
  (54 shorter events, 0.7 us)
Async XLA Ops:
  0.0 29.1 %copy-start = (f32[8,1024]{1,0:T(8,128)S(1)}, f32[8,1024]{1,0:T(8,128)}, u32[]{:S(2)}) copy-start(f32[8,1024]{1,0:T(8,128)} %param.13) | copy-start | bytes 98308
  0.0 8.3 %copy-start.3 = (s32[128]{0:T(128)S(1)}, s32[128]{0:T(128)}, u32[]{:S(2)}) copy-start(s32[128]{0:T(128)} %param.15) | copy-start | bytes 1540
  0.0 29.0 %copy-start.2 = (f32[3,3,1024]{2,1,0:T(4,128)S(1)}, f32[3,3,1024]{2,1,0:T(4,128)}, u32[]{:S(2)}) copy-start(f32[3,3,1024]{2,1,0:T(4,128)} %param.11) | copy-start | bytes 110596
  4.0 25.7 %collective-permute-start = (bf16[3,2,1024]{2,1,0:T(2,128)(2,1)S(1)}, bf16[3,2,1024]{2,1,0:T(2,128)(2,1)S(1)}, u32[]{:S(2)}, u32[]{:S(2)}) collective-permute-start(bf16[3,2,1024]{2,1,0:T(2,128)(2,1)S(1)} %copy.58), channel_id=1, source_target_pairs={{0,8},{8,16},{16,24},{24,32},{32,40},{40,48},{48,56},{56,64},{64,7... | collective-permute-start | bytes 36872 | tf_op jit(solution)/shard_map/ppermute | solution.py:10
  8.4 21.2 %collective-permute-start.1 = (s32[2]{0:T(128)S(1)}, s32[2]{0:T(128)S(1)}, u32[]{:S(2)}, u32[]{:S(2)}) collective-permute-start(s32[2]{0:T(128)S(1)} %slice.217), channel_id=1, source_target_pairs={{0,8},{8,16},{16,24},{24,32},{32,40},{40,48},{48,56},{56,64},{64,7... | collective-permute-start | bytes 32 | tf_op jit(solution)/shard_map/ppermute | solution.py:10
  13.3 26.8 %all-to-all-start = ((s32[64,1,128]{2,1,0:T(1,128)}), s32[64,1,128]{2,1,0:T(1,128)S(1)}, u32[]{:S(2)}, u32[]{:S(2)}) async-start(s32[64,1,128]{2,1,0:T(1,128)} %stack.14), calls=%async_computation | async-start | bytes 65536 | tf_op jit(solution)/shard_map/all_to_all | solution.py:79
  40.0 20.5 %all-to-all-start.1 = ((bf16[128,64,16]{0,2,1:T(8,128)(2,1)}), bf16[128,64,16]{0,2,1:T(8,128)(2,1)S(1)}, u32[]{:S(2)}, u32[]{:S(2)}) async-start(bf16[128,64,16]{0,2,1:T(8,128)(2,1)} %bitcast.5), calls=%async_computation.1 | async-start | bytes 524288 | tf_op jit(solution)/shard_map/all_to_all | solution.py:77
  144.2 22.2 %copy-start.4 = (f32[1024]{0:T(1024)S(1)}, f32[1024]{0:T(1024)}, u32[]{:S(2)}) copy-start(f32[1024]{0:T(1024)} %param.14) | copy-start | bytes 12292
  144.9 22.6 %copy-start.1 = (f32[8,1024]{1,0:T(8,128)S(1)}, f32[8,1024]{1,0:T(8,128)}, u32[]{:S(2)}) copy-start(f32[8,1024]{1,0:T(8,128)} %param.13) | copy-start | bytes 98308
